TPU v7x, 32 devices: a whole 2x2x4 slice. The times are simulated.
32 devices in a mesh: space: 16 (over z, y, x), src: 2 (over core).
Axes of the slice: x: 2, y: 2, z: 4, core: 2. Of those that a mesh axis runs over, the one named last changes fastest.
Arguments:
- rhs: float32 [12288, 1024], P('space', 'src'), may hold values from -18 to 18
- diag_blocks: bfloat16 [48, 256, 256], P('space', 'src'), may hold values from -0.5 to 5.5
- couple_blocks: bfloat16 [48, 2, 256, 256], P('space', None, 'src'), may hold values from -0.1875 to 0.1875
- halo_weight: bfloat16 [32, 256, 128], P('space', 'src'), may hold values from -0.25 to 0.25
- neighbours: int32 [48, 2], P('space'), may hold values from 0 to 2
- boundary: int32 [32, 128], P('space'), may hold values from 0 to 767
Outputs:
- solution: float32 [12288, 1024], P('space', 'src')
- misfit: float32 [1024], P('src')
All inputs are finite; a program needn't handle non-finite values.
Results may differ from a plain program's by a relative error of at most 0.0032.
Values may be sent and summed in bfloat16 or wider, within the bound.
A program may use at most 64 MiB of HBM per device.

v0:
```python
import functools

import jax
import jax.numpy as jnp
from jax import lax
from jax.experimental import pallas as pl
from jax.experimental.pallas import tpu as pltpu
from jax.sharding import PartitionSpec as P

SWEEPS = 4
CHUNKS = 4
GROUP = 1
MESH = pl.DeviceIdType.MESH

centre = 4.0
half_width = 2.0


def sweep_weights():
    sigma = centre / half_width
    ratio = 1.0 / sigma
    weights = []
    for _ in range(SWEEPS - 1):
        ratio_new = 1.0 / (2.0 * sigma - ratio)
        weights.append((ratio_new * ratio, 2.0 * ratio_new / half_width))
        ratio = ratio_new
    return weights


def kernel(
    n_space, n_src,
    rhs_ref, diag_ref, couple_ref, halo_ref, nbr_ref, bnd_ref,
    total, misfit_ref,
    res, dirn, rounded, weights, gmat, picks, bounds, outbox, inbox, red_b, red_r,
    rhs_sem, bnd_sem, own_sem, op_send, op_recv, halo_send, halo_recv, sums_send, sums_recv, heard,
):
    me = lax.axis_index("space")
    core = lax.axis_index("src")
    aggs, size, depth = weights.shape
    edges, width = res.shape
    nbrs = couple_ref.shape[1]
    halo = bnd_ref.shape[1]
    part = size // n_src
    cols = width // CHUNKS

    def span(c, many=1):
        return pl.ds(c * cols, many * cols)

    rhs_loads = [
        pltpu.make_async_copy(rhs_ref.at[:, span(c)], res.at[:, span(c)], rhs_sem.at[c])
        for c in range(CHUNKS)
    ]
    bnd_load = pltpu.make_async_copy(bnd_ref, bounds, bnd_sem)
    bnd_load.start()
    for load in rhs_loads:
        load.start()
    rows = pl.ds(pl.multiple_of(core * part, part), part)
    pieces = [(diag_ref, weights.at[:, rows, pl.ds(0, size)])]
    for k in range(nbrs):
        pieces.append((couple_ref.at[:, k], weights.at[:, rows, pl.ds((k + 1) * size, size)]))
    pieces.append((halo_ref, gmat.at[:, rows]))
    own = [pltpu.make_async_copy(a, b, own_sem.at[i]) for i, (a, b) in enumerate(pieces)]
    for load in own:
        load.start()

    barrier = pltpu.get_barrier_semaphore()

    def greet(axis, to):
        pl.semaphore_signal(barrier, inc=1, device_id={axis: to}, device_id_type=MESH)

    def across(j):
        return me + (1 - 2 * (lax.div(me, 1 << j) % 2)) * (1 << j)

    rounds = []
    if n_space & (n_space - 1) == 0:
        dims = n_space.bit_length() - 1
        for j in range(dims):
            greet("space", across(j))
        pl.when(me > 0)(lambda: greet("space", me - 1))
        pl.when(me < n_space - 1)(lambda: greet("space", me + 1))
        greeted = dims + (me > 0).astype(jnp.int32) + (me < n_space - 1).astype(jnp.int32)
        rounds = list(range(1, dims))
    else:

        @pl.loop(1, n_space)
        def _(k):
            greet("space", lax.rem(me + k, n_space))

        greeted = n_space - 1
    for k in range(1, n_src):
        greet("src", lax.rem(core + k, n_src))

    def hear(j):
        if j > 1:
            pl.semaphore_wait(heard.at[j - 1], 1)
        pl.semaphore_signal(
            heard.at[j], inc=1, device_id={"space": across(j)}, device_id_type=MESH
        )

    last_round = rounds[-1] if rounds else None

    bnd_load.wait()
    at = lax.broadcasted_iota(jnp.int32, (edges, halo), 0)
    for i, side in enumerate((1, 0)):
        hit = (at == bounds[side : side + 1, :]).astype(jnp.float32)
        picks[pl.ds(i * halo, halo), :] = hit.T.astype(jnp.bfloat16)

    @pl.when(me == 0)
    def _():
        inbox[:, :, 0] = jnp.zeros_like(inbox[:, :, 0])

    @pl.when(me == n_space - 1)
    def _():
        inbox[:, :, 1] = jnp.zeros_like(inbox[:, :, 1])

    def pack(s, c):
        picked = jnp.dot(picks[...], rounded[:, :, span(c)].reshape(edges, cols), preferred_element_type=jnp.float32)
        outbox[s, c] = picked.astype(jnp.bfloat16).reshape(2, halo, cols)

    def passed(s, c, side):
        to = lax.rem(me + 1, n_space) if side == 0 else lax.rem(me + n_space - 1, n_space)
        return pltpu.make_async_remote_copy(
            src_ref=outbox.at[s, c, side],
            dst_ref=inbox.at[s, c, side],
            send_sem=halo_send.at[s, c, side],
            recv_sem=halo_recv.at[s, c, side],
            device_id={"space": to},
            device_id_type=MESH,
        )

    sends = (me < n_space - 1, me > 0)
    takes = (me > 0, me < n_space - 1)

    def send(s, c):
        for side in range(2):
            pl.when(sends[side])(passed(s, c, side).start)

    def take(s, c):
        for side in range(2):
            pl.when(takes[side])(passed(s, c, side).wait_recv)

    def share(buffer, index):
        def one(k, carry):
            pltpu.make_async_remote_copy(
                src_ref=buffer.at[me],
                dst_ref=buffer.at[me],
                send_sem=sums_send.at[index],
                recv_sem=sums_recv.at[index],
                device_id={"space": lax.rem(me + k, n_space)},
                device_id_type=MESH,
            ).start()
            return carry

        lax.fori_loop(1, n_space, one, 0)

    def collected(buffer, sem):
        others = buffer.at[pl.ds(0, n_space - 1)]
        pltpu.make_async_copy(others, others, sem).wait()

    for c in range(CHUNKS):
        rhs_loads[c].wait()
        right = res[:, span(c)]
        start = right / centre
        dirn[:, span(c)] = start
        rounded[:, :, span(c)] = start.astype(jnp.bfloat16).reshape(aggs, size, cols)
        pack(0, c)
        if c == 0:
            pl.semaphore_wait(barrier, greeted + n_src - 1)
        send(0, c)
        red_b[me, :, span(c)] = jnp.sum(right * right, axis=0, keepdims=True)

    moves = []
    for k in range(1, n_src):
        for i, (a, b) in enumerate(pieces):
            move = pltpu.make_async_remote_copy(
                src_ref=a,
                dst_ref=b,
                send_sem=op_send.at[k - 1, i],
                recv_sem=op_recv.at[k - 1, i],
                device_id={"src": lax.rem(core + k, n_src)},
                device_id_type=MESH,
            )
            move.start()
            moves.append(move)
    if rounds:
        hear(rounds.pop(0))
    for load in own:
        load.wait()
    for move in moves:
        move.wait()

    def local_part(c):
        wide = span(c, GROUP)
        for a in range(aggs):
            group = pl.ds(a * size, size)
            beside = [rounded[a, :, wide]]
            for k in range(nbrs):
                beside.append(rounded[nbr_ref[k, a], :, wide])
            res[group, wide] -= jnp.dot(
                weights[a], jnp.concatenate(beside, axis=0), preferred_element_type=jnp.float32
            )

    def halo_part(s, c):
        for side, a in ((0, 0), (1, aggs - 1)):
            group = pl.ds(a * size, size)
            res[group, span(c)] -= jnp.dot(
                gmat[side], inbox[s, c, side], preferred_element_type=jnp.float32
            )

    for c in range(0, CHUNKS, GROUP):
        local_part(c)

    steps = sweep_weights()
    for s in range(SWEEPS - 1):
        keep, gain = steps[s]
        for c in range(CHUNKS):
            take(s, c)
            halo_part(s, c)
            before = dirn[:, span(c)]
            after = keep * before + gain * res[:, span(c)]
            rounded[:, :, span(c)] = after.astype(jnp.bfloat16).reshape(aggs, size, cols)
            pack(s + 1, c)
            send(s + 1, c)
            dirn[:, span(c)] = after
            if s == 0:
                total[:, span(c)] = before + after
            else:
                total[:, span(c)] += after
            if (c + 1) % GROUP == 0:
                local_part(c + 1 - GROUP)
                if rounds:
                    hear(rounds.pop(0))

    assert not rounds
    if last_round is not None:
        pl.semaphore_wait(heard.at[last_round], 1)
    share(red_b, 0)
    for c in range(CHUNKS):
        take(SWEEPS - 1, c)
        halo_part(SWEEPS - 1, c)
        left = res[:, span(c)]
        red_r[me, :, span(c)] = jnp.sum(left * left, axis=0, keepdims=True)
    share(red_r, 1)
    collected(red_b, sums_recv.at[0])
    bb = jnp.sum(red_b[...], axis=0)
    for s in range(SWEEPS):
        for c in range(CHUNKS):
            for side in range(2):
                pl.when(sends[side])(passed(s, c, side).wait_send)
    collected(red_b, sums_send.at[0])
    collected(red_r, sums_recv.at[1])
    rr = jnp.sum(red_r[...], axis=0)
    misfit_ref[...] = jnp.sqrt(rr / (bb + 1e-06))
    collected(red_r, sums_send.at[1])


def local(n_space, n_src, rhs, diag_blocks, couple_blocks, halo_weight, neighbours, boundary):
    edges, width = rhs.shape
    aggs, part, size = diag_blocks.shape
    nbrs = couple_blocks.shape[1]
    halo = boundary.shape[1]
    cols = width // CHUNKS
    bf16, f32 = jnp.bfloat16, jnp.float32
    dma = pltpu.SemaphoreType.DMA
    outside = pl.BlockSpec(memory_space=pltpu.HBM)
    inside = pl.BlockSpec(memory_space=pltpu.VMEM)
    result, misfit = pl.pallas_call(
        functools.partial(kernel, n_space, n_src),
        out_shape=(
            pltpu.VMEM((edges, width), f32),
            jax.ShapeDtypeStruct((1, width), f32),
        ),
        in_specs=[outside] * 4 + [pl.BlockSpec(memory_space=pltpu.SMEM), outside],
        out_specs=(pl.BlockSpec(memory_space=pltpu.VMEM), inside),
        scratch_shapes=[
            pltpu.VMEM((edges, width), f32),
            pltpu.VMEM((edges, width), f32),
            pltpu.VMEM((aggs, size, width), bf16),
            pltpu.VMEM((aggs, size, (nbrs + 1) * size), bf16),
            pltpu.VMEM((2, size, halo), bf16),
            pltpu.VMEM((2 * halo, edges), bf16),
            pltpu.VMEM((2, halo), jnp.int32),
            pltpu.VMEM((SWEEPS, CHUNKS, 2, halo, cols), bf16),
            pltpu.VMEM((SWEEPS, CHUNKS, 2, halo, cols), bf16),
            pltpu.VMEM((n_space, 1, width), f32),
            pltpu.VMEM((n_space, 1, width), f32),
            dma((CHUNKS,)),
            dma,
            dma((nbrs + 2,)),
            dma((max(n_src - 1, 1), nbrs + 2)),
            dma((max(n_src - 1, 1), nbrs + 2)),
            dma((SWEEPS, CHUNKS, 2)),
            dma((SWEEPS, CHUNKS, 2)),
            dma((2,)),
            dma((2,)),
            pltpu.SemaphoreType.REGULAR((max(n_space.bit_length() - 1, 1),)),
        ],
        compiler_params=pltpu.CompilerParams(
            collective_id=0, has_side_effects=True, vmem_limit_bytes=67043328 - edges * width * 4
        ),
    )(rhs, diag_blocks, couple_blocks, halo_weight, neighbours.T, boundary)
    return result, misfit.reshape(width)


def solution(mesh):
    placed = (
        P("space", "src"),
        P("space", "src", None),
        P("space", None, "src", None),
        P("space", "src", None),
        P("space", None),
        P("space", None),
    )
    body = functools.partial(local, mesh.shape["space"], mesh.shape["src"])
    return jax.shard_map(
        body, mesh=mesh, in_specs=placed, out_specs=(P("space", "src"), P("src")), check_vma=False
    )
```

profile of v0, /device:TPU:0, one launch (start us, length us, event | category | flops | bytes accessed | tf_op | source)
XLA Modules:
  0.0 39.5 jit_solution(5651221745549484238)
XLA Ops:
  0.6 37.1 %shard_map.77 = (f32[768,512]{1,0:T(8,128)S(1)}, f32[1,512]{1,0:T(1,128)}) custom-call(f32[768,512]{1,0:T(8,128)} %rhs_ref.1, bf16[3,128,256]{2,1,0:T(8,128)(2,1)} %diag_ref.1, bf16[3,2,128,256]{3,2,1,0:T(8,128)(2,1)} %couple_ref.1, bf16[2,128,128]{2,1,0:T(8,128)(2,1)} %halo_ref.1, s32[2,3]{1,0:T(2,128)} %bitcast.3, s32[2,128]{1,0:T(2,128)} %bnd_ref.1), custom_call_target="tpu_custom_call" | custom-call | tf_op jit(solution)/shard_map/pallas_call | solution.py:267
  37.8 0.0 copy-start
  37.8 1.1 %copy.10 = f32[768,512]{1,0:T(8,128)} copy(f32[768,512]{1,0:T(8,128)S(1)} %get-tuple-element.6) | data formatting | bytes 3145728
  38.9 0.0 copy-done
  38.9 0.6 %copy.11 = f32[512]{0:T(512)} copy(f32[512]{0:T(512)S(1)} %bitcast.2) | data formatting | bytes 4096
Async XLA Ops:
  37.8 1.2 %copy-start = (f32[1,512]{1,0:T(1,128)S(1)}, f32[1,512]{1,0:T(1,128)}, u32[]{:S(2)}) copy-start(f32[1,512]{1,0:T(1,128)} %get-tuple-element.5) | copy-start | bytes 6148
where the time goes:
time: 39.7 us; the launch traced here: 39.5 us
  Pallas kernels  37.1 us (93%)
  local copies, waits for them, and re-layouts  1.73 us (4%)
  between operations  0.65 us (2%)
    pallas_call x1, Pallas kernels, local(): pl.pallas_call(functools.partial(kernel, n_space, n_src), out_shape=(pltp...  37.1 us
    unnamed x4, local copies, waits for them, and re-layouts  1.73 us

commit v1 on v0

v1 whole, which is shorter than its diff:
```python
import functools

import jax
import jax.numpy as jnp
from jax import lax
from jax.experimental import pallas as pl
from jax.experimental.pallas import tpu as pltpu
from jax.sharding import PartitionSpec as P

SWEEPS = 4
CHUNKS = 4
GROUP = 1
MESH = pl.DeviceIdType.MESH

centre = 4.0
half_width = 2.0


def sweep_weights():
    sigma = centre / half_width
    ratio = 1.0 / sigma
    weights = []
    for _ in range(SWEEPS - 1):
        ratio_new = 1.0 / (2.0 * sigma - ratio)
        weights.append((ratio_new * ratio, 2.0 * ratio_new / half_width))
        ratio = ratio_new
    return weights


def kernel(
    n_space, n_src,
    rhs_ref, diag_ref, couple_ref, halo_ref, nbr_hbm, bnd_ref,
    total, misfit_ref,
    res, dirn, rounded, weights, gmat, picks, spread, ahead, bounds, nbr_ref, outbox, inbox, red,
    rhs_sem, bnd_sem, nbr_sem, own_sem, op_send, op_recv, halo_send, halo_recv, sums_send, sums_recv, heard,
):
    me = lax.axis_index("space")
    core = lax.axis_index("src")
    aggs, size, depth = weights.shape
    edges, width = res.shape
    nbrs = couple_ref.shape[1]
    halo = bnd_ref.shape[1]
    part = size // n_src
    cols = width // CHUNKS
    bf16, f32 = jnp.bfloat16, jnp.float32

    def span(c, many=1):
        return pl.ds(c * cols, many * cols)

    def rows(a):
        return pl.ds(a * size, size)

    def dot(a, b):
        return jnp.dot(a, b, preferred_element_type=f32)

    rhs_loads = [
        pltpu.make_async_copy(rhs_ref.at[:, span(c)], res.at[:, span(c)], rhs_sem.at[c])
        for c in range(CHUNKS)
    ]
    bnd_load = pltpu.make_async_copy(bnd_ref, bounds, bnd_sem)
    bnd_load.start()
    for load in rhs_loads:
        load.start()
    mine = pl.ds(pl.multiple_of(core * part, part), part)
    pieces = [(diag_ref, weights.at[:, mine, pl.ds(0, size)])]
    for k in range(nbrs):
        pieces.append((couple_ref.at[:, k], weights.at[:, mine, pl.ds((k + 1) * size, size)]))
    pieces.append((halo_ref, gmat.at[:, mine]))
    own = [pltpu.make_async_copy(a, b, own_sem.at[i]) for i, (a, b) in enumerate(pieces)]
    nbr_load = pltpu.make_async_copy(nbr_hbm, nbr_ref, nbr_sem)
    nbr_load.start()
    for load in own:
        load.start()

    barrier = pltpu.get_barrier_semaphore()

    def greet(axis, to):
        pl.semaphore_signal(barrier, inc=1, device_id={axis: to}, device_id_type=MESH)

    def across(j):
        return me + (1 - 2 * (lax.div(me, 1 << j) % 2)) * (1 << j)

    hears = []
    if n_space & (n_space - 1) == 0:
        dims = n_space.bit_length() - 1
        for j in range(dims):
            greet("space", across(j))
        pl.when(me > 0)(lambda: greet("space", me - 1))
        pl.when(me < n_space - 1)(lambda: greet("space", me + 1))
        greeted = dims + (me > 0).astype(jnp.int32) + (me < n_space - 1).astype(jnp.int32)
        hears = list(range(1, dims))
    else:

        @pl.loop(1, n_space)
        def _(k):
            greet("space", lax.rem(me + k, n_space))

        greeted = n_space - 1
    for k in range(1, n_src):
        greet("src", lax.rem(core + k, n_src))

    last_heard = hears[-1] if hears else None

    def hear():
        j = hears.pop(0)
        if j > 1:
            pl.semaphore_wait(heard.at[j - 1], 1)
        pl.semaphore_signal(
            heard.at[j], inc=1, device_id={"space": across(j)}, device_id_type=MESH
        )

    bnd_load.wait()
    diagonal = lax.broadcasted_iota(jnp.int32, (halo, halo), 0) == lax.broadcasted_iota(
        jnp.int32, (halo, halo), 1
    )
    at = lax.broadcasted_iota(jnp.int32, (halo, edges), 1)
    for i, side in enumerate((1, 0)):
        listed = bounds[side : side + 1, :].astype(f32)
        column = jnp.sum(jnp.where(diagonal, listed, 0.0), axis=1, keepdims=True).astype(jnp.int32)
        picks[pl.ds(i * halo, halo), :] = (at == column).astype(f32).astype(bf16)

    @pl.when(me == 0)
    def _():
        inbox[:, :, 0] = jnp.zeros_like(inbox[:, :, 0])

    @pl.when(me == n_space - 1)
    def _():
        inbox[:, :, 1] = jnp.zeros_like(inbox[:, :, 1])

    def passed(s, c, side):
        to = lax.rem(me + 1, n_space) if side == 0 else lax.rem(me + n_space - 1, n_space)
        return pltpu.make_async_remote_copy(
            src_ref=outbox.at[s, c, side],
            dst_ref=inbox.at[s, c, side],
            send_sem=halo_send.at[s, c, side],
            recv_sem=halo_recv.at[s, c, side],
            device_id={"space": to},
            device_id_type=MESH,
        )

    sends = (me < n_space - 1, me > 0)
    takes = (me > 0, me < n_space - 1)

    def send(s, c):
        for side in range(2):
            pl.when(sends[side])(passed(s, c, side).start)

    def take(s, c):
        for side in range(2):
            pl.when(takes[side])(passed(s, c, side).wait_recv)

    moves = [
        pltpu.make_async_remote_copy(
            src_ref=a,
            dst_ref=b,
            send_sem=op_send.at[k - 1, i],
            recv_sem=op_recv.at[k - 1, i],
            device_id={"src": lax.rem(core + k, n_src)},
            device_id_type=MESH,
        )
        for k in range(1, n_src)
        for i, (a, b) in enumerate(pieces)
    ]

    for c in range(CHUNKS):
        rhs_loads[c].wait()
        right = res[:, span(c)]
        start = right * (1.0 / centre)
        dirn[:, span(c)] = start
        total[:, span(c)] = start
        first = start.astype(bf16)
        rounded[0, :, :, span(c)] = first.reshape(aggs, size, cols)
        outbox[0, c] = dot(picks[...], first).astype(bf16).reshape(2, halo, cols)
        if c == 0:
            pl.semaphore_wait(barrier, greeted + n_src - 1)
        send(0, c)
        if c == 0:
            for move in moves:
                move.start()
        red[me, 0:1, span(c)] = jnp.sum(right * right, axis=0, keepdims=True)

    if hears:
        hear()
    nbr_load.wait()
    for load in own:
        load.wait()
    for move in moves:
        move.wait()
    for side, a in ((0, 0), (1, aggs - 1)):
        spread[:, pl.ds(side * halo, halo)] = dot(picks[:, rows(a)], gmat[side]).astype(bf16)

    def local_part(c, now, later, keep, gain):
        wide = span(c, GROUP)
        ready = []
        for a in range(aggs):
            beside = [rounded[now, a, :, wide]]
            for k in range(nbrs):
                beside.append(rounded[now, nbr_ref[k, a], :, wide])
            left = res[rows(a), wide] - dot(weights[a], jnp.concatenate(beside, axis=0))
            res[rows(a), wide] = left
            if keep is not None:
                onward = keep * dirn[rows(a), wide] + gain * left
                dirn[rows(a), wide] = onward
                rounded[later, a, :, wide] = onward.astype(bf16)
                if 0 < a < aggs - 1:
                    total[rows(a), wide] += onward
        if keep is not None:
            ahead[:, wide] = dot(picks[...], rounded[later, :, :, wide].reshape(edges, GROUP * cols))

    def halo_part(s, c, later, gain):
        take(s, c)
        came = inbox[s, c].reshape(2 * halo, cols)
        onward = ahead[:, span(c)] - gain * dot(spread[...], came)
        outbox[s + 1, c] = onward.astype(bf16).reshape(2, halo, cols)
        send(s + 1, c)
        for side, a in ((0, 0), (1, aggs - 1)):
            pushed = dot(gmat[side], inbox[s, c, side])
            res[rows(a), span(c)] -= pushed
            step = dirn[rows(a), span(c)] - gain * pushed
            dirn[rows(a), span(c)] = step
            total[rows(a), span(c)] += step
            rounded[later, a, :, span(c)] = step.astype(bf16)

    steps = sweep_weights()
    for c in range(0, CHUNKS, GROUP):
        local_part(c, 0, 1, *steps[0])
    if hears:
        hear()
    for s in range(SWEEPS - 1):
        for c in range(CHUNKS):
            halo_part(s, c, (s + 1) % 2, steps[s][1])
            if (c + 1) % GROUP == 0:
                local_part(c + 1 - GROUP, (s + 1) % 2, s % 2, *(steps[s + 1] if s + 2 < SWEEPS else (None, None)))

    while hears:
        hear()
    for c in range(CHUNKS):
        take(SWEEPS - 1, c)
        squares = jnp.zeros((1, cols), f32)
        for a in range(aggs):
            left = res[rows(a), span(c)]
            for side, b in ((0, 0), (1, aggs - 1)):
                if a == b:
                    left = left - dot(gmat[side], inbox[SWEEPS - 1, c, side])
            squares = squares + jnp.sum(left * left, axis=0, keepdims=True)
        red[me, 1:2, span(c)] = squares
    if last_heard is not None:
        pl.semaphore_wait(heard.at[last_heard], 1)

    def share(k, carry):
        pltpu.make_async_remote_copy(
            src_ref=red.at[me],
            dst_ref=red.at[me],
            send_sem=sums_send,
            recv_sem=sums_recv,
            device_id={"space": lax.rem(me + k, n_space)},
            device_id_type=MESH,
        ).start()
        return carry

    lax.fori_loop(1, n_space, share, 0)
    for s in range(SWEEPS):
        for c in range(CHUNKS):
            for side in range(2):
                pl.when(sends[side])(passed(s, c, side).wait_send)
    others = red.at[pl.ds(0, n_space - 1)]
    pltpu.make_async_copy(others, others, sums_recv).wait()
    sums = jnp.sum(red[...], axis=0)
    misfit_ref[...] = jnp.sqrt(sums[1:2] / (sums[0:1] + 1e-06))
    pltpu.make_async_copy(others, others, sums_send).wait()


def store(total, misfit_ref, out, misfit_out, flat, sems):
    rows = total.shape[0] // CHUNKS
    copies = [
        pltpu.make_async_copy(total.at[pl.ds(c * rows, rows)], out.at[pl.ds(c * rows, rows)], sems.at[c])
        for c in range(CHUNKS)
    ]
    for copy in copies:
        copy.start()
    flat[...] = misfit_ref[0, :]
    copies.append(pltpu.make_async_copy(flat, misfit_out, sems.at[CHUNKS]))
    copies[-1].start()
    for copy in copies:
        copy.wait()


def local(n_space, n_src, rhs, diag_blocks, couple_blocks, halo_weight, neighbours, boundary):
    edges, width = rhs.shape
    aggs, part, size = diag_blocks.shape
    nbrs = couple_blocks.shape[1]
    halo = boundary.shape[1]
    cols = width // CHUNKS
    bf16, f32 = jnp.bfloat16, jnp.float32
    dma = pltpu.SemaphoreType.DMA
    outside = pl.BlockSpec(memory_space=pltpu.HBM)
    inside = pl.BlockSpec(memory_space=pltpu.VMEM)
    result, misfit = pl.pallas_call(
        functools.partial(kernel, n_space, n_src),
        out_shape=(
            pltpu.VMEM((edges, width), f32),
            pltpu.VMEM((1, width), f32),
        ),
        in_specs=[outside] * 6,
        out_specs=(inside, inside),
        scratch_shapes=[
            pltpu.VMEM((edges, width), f32),
            pltpu.VMEM((edges, width), f32),
            pltpu.VMEM((2, aggs, size, width), bf16),
            pltpu.VMEM((aggs, size, (nbrs + 1) * size), bf16),
            pltpu.VMEM((2, size, halo), bf16),
            pltpu.VMEM((2 * halo, edges), bf16),
            pltpu.VMEM((2 * halo, 2 * halo), bf16),
            pltpu.VMEM((2 * halo, width), f32),
            pltpu.VMEM((2, halo), jnp.int32),
            pltpu.SMEM((nbrs, aggs), jnp.int32),
            pltpu.VMEM((SWEEPS, CHUNKS, 2, halo, cols), bf16),
            pltpu.VMEM((SWEEPS, CHUNKS, 2, halo, cols), bf16),
            pltpu.VMEM((n_space, 2, width), f32),
            dma((CHUNKS,)),
            dma,
            dma,
            dma((nbrs + 2,)),
            dma((max(n_src - 1, 1), nbrs + 2)),
            dma((max(n_src - 1, 1), nbrs + 2)),
            dma((SWEEPS, CHUNKS, 2)),
            dma((SWEEPS, CHUNKS, 2)),
            dma,
            dma,
            pltpu.SemaphoreType.REGULAR((max(n_space.bit_length() - 1, 1),)),
        ],
        compiler_params=pltpu.CompilerParams(
            collective_id=0, has_side_effects=True, vmem_limit_bytes=(60 << 20) - edges * width * 4
        ),
    )(rhs, diag_blocks, couple_blocks, halo_weight, neighbours.T, boundary)
    return pl.pallas_call(
        store,
        out_shape=(
            jax.ShapeDtypeStruct((edges, width), f32),
            jax.ShapeDtypeStruct((width,), f32),
        ),
        in_specs=[inside, inside],
        out_specs=(outside, outside),
        scratch_shapes=[pltpu.VMEM((width,), f32), dma((CHUNKS + 1,))],
    )(
        pltpu.with_memory_space_constraint(result, pltpu.VMEM),
        pltpu.with_memory_space_constraint(misfit, pltpu.VMEM),
    )


def solution(mesh):
    placed = (
        P("space", "src"),
        P("space", "src", None),
        P("space", None, "src", None),
        P("space", "src", None),
        P("space", None),
        P("space", None),
    )
    body = functools.partial(local, mesh.shape["space"], mesh.shape["src"])
    return jax.shard_map(
        body, mesh=mesh, in_specs=placed, out_specs=(P("space", "src"), P("src")), check_vma=False
    )
```

time: 39.7 us -> 37.3 us (0.940)
  local copies, waits for them, and re-layouts: 1.73 us -> 0 us
  Pallas kernels: 37.1 us -> 36.5 us
    pallas_call x1, Pallas kernels: 37.1 us -> 35.3 us  [local(): pl.pallas_call(functools.partial(kernel, n_space, n_src), out_shape=(pltp...]
    unnamed x4 -> x0, local copies, waits for them, and re-layouts: 1.73 us -> none
    pallas_call x0 -> x1, Pallas kernels: none -> 1.18 us  [local(): pl.pallas_call(store, out_shape=(jax.ShapeDtypeStruct((edges, width), f32...]
where the time goes in v1:
time: 37.3 us; the launch traced here: 37.2 us
  Pallas kernels  36.5 us (98%)
  between operations  0.64 us (2%)
    pallas_call x1, Pallas kernels, local(): pl.pallas_call(functools.partial(kernel, n_space, n_src), out_shape=(pltp...  35.3 us
    pallas_call x1, Pallas kernels, local(): pl.pallas_call(store, out_shape=(jax.ShapeDtypeStruct((edges, width), f32...  1.18 us

profile of v1, /device:TPU:0, one launch (start us, length us, event | category | flops | bytes accessed | tf_op | source)
XLA Modules:
  0.0 37.2 jit_solution(1194439854821062185)
XLA Ops:
  0.6 35.3 %shard_map.77 = (f32[768,512]{1,0:T(8,128)S(1)}, f32[1,512]{1,0:T(1,128)S(1)}) custom-call(f32[768,512]{1,0:T(8,128)} %rhs_ref.1, bf16[3,128,256]{2,1,0:T(8,128)(2,1)} %diag_ref.1, bf16[3,2,128,256]{3,2,1,0:T(8,128)(2,1)} %couple_ref.1, bf16[2,128,128]{2,1,0:T(8,128)(2,1)} %halo_ref.1, s32[2,3]{1,0:T(2,128)} %bitcast.1, s32[2,128]{1,0:T(2,128)} %bnd_ref.1), custom_call_target="tpu_custom_call" | custom-call | tf_op jit(solution)/shard_map/pallas_call | solution.py:298
  36.0 1.2 %shard_map.78 = (f32[768,512]{1,0:T(8,128)}, f32[512]{0:T(512)}) custom-call(f32[768,512]{1,0:T(8,128)S(1)} %get-tuple-element.4.total, f32[1,512]{1,0:T(1,128)S(1)} %get-tuple-element.5.misfit_ref), custom_call_target="tpu_custom_call" | custom-call | tf_op jit(solution)/shard_map/pallas_call | solution.py:336

commit v2 on v1

--- a/solution.py
+++ b/solution.py
@@ -57,9 +57,25 @@
         pltpu.make_async_copy(rhs_ref.at[:, span(c)], res.at[:, span(c)], rhs_sem.at[c])
         for c in range(CHUNKS)
     ]
+    barrier = pltpu.get_barrier_semaphore()
+
+    def greet(axis, to):
+        pl.semaphore_signal(barrier, inc=1, device_id={axis: to}, device_id_type=MESH)
+
+    def within(step):
+        return ((me >= step, me - step), (me < n_space - step, me + step))
+
+    def count(step):
+        return sum(there.astype(jnp.int32) for there, _ in within(step))
+
+    rhs_loads[0].start()
     bnd_load = pltpu.make_async_copy(bnd_ref, bounds, bnd_sem)
     bnd_load.start()
-    for load in rhs_loads:
+    for there, to in within(1):
+        pl.when(there)(functools.partial(greet, "space", to))
+    for k in range(1, n_src):
+        greet("src", lax.rem(core + k, n_src))
+    for load in rhs_loads[1:]:
         load.start()
     mine = pl.ds(pl.multiple_of(core * part, part), part)
     pieces = [(diag_ref, weights.at[:, mine, pl.ds(0, size)])]
@@ -72,42 +88,30 @@
     for load in own:
         load.start()
 
-    barrier = pltpu.get_barrier_semaphore()
-
-    def greet(axis, to):
-        pl.semaphore_signal(barrier, inc=1, device_id={axis: to}, device_id_type=MESH)
-
-    def across(j):
-        return me + (1 - 2 * (lax.div(me, 1 << j) % 2)) * (1 << j)
-
-    hears = []
-    if n_space & (n_space - 1) == 0:
-        dims = n_space.bit_length() - 1
-        for j in range(dims):
-            greet("space", across(j))
-        pl.when(me > 0)(lambda: greet("space", me - 1))
-        pl.when(me < n_space - 1)(lambda: greet("space", me + 1))
-        greeted = dims + (me > 0).astype(jnp.int32) + (me < n_space - 1).astype(jnp.int32)
-        hears = list(range(1, dims))
-    else:
-
-        @pl.loop(1, n_space)
-        def _(k):
-            greet("space", lax.rem(me + k, n_space))
-
-        greeted = n_space - 1
-    for k in range(1, n_src):
-        greet("src", lax.rem(core + k, n_src))
-
-    last_heard = hears[-1] if hears else None
-
-    def hear():
-        j = hears.pop(0)
-        if j > 1:
-            pl.semaphore_wait(heard.at[j - 1], 1)
-        pl.semaphore_signal(
-            heard.at[j], inc=1, device_id={"space": across(j)}, device_id_type=MESH
-        )
+    levels = (n_space - 1).bit_length()
+    told = []
+
+    def tell():
+        j = len(told)
+        if j > levels:
+            return
+        if j > 0:
+            known = count(1 << (j - 1))
+
+            @pl.when(known > 0)
+            def _():
+                pl.semaphore_wait(heard.at[j - 1], known)
+
+        if j < levels:
+            for there, to in within(1 << j):
+
+                @pl.when(there)
+                def _():
+                    pl.semaphore_signal(
+                        heard.at[j], inc=1, device_id={"space": to}, device_id_type=MESH
+                    )
+
+        told.append(j)
 
     bnd_load.wait()
     diagonal = lax.broadcasted_iota(jnp.int32, (halo, halo), 0) == lax.broadcasted_iota(
@@ -127,27 +131,30 @@
     def _():
         inbox[:, :, 1] = jnp.zeros_like(inbox[:, :, 1])
 
-    def passed(s, c, side):
-        to = lax.rem(me + 1, n_space) if side == 0 else lax.rem(me + n_space - 1, n_space)
-        return pltpu.make_async_remote_copy(
-            src_ref=outbox.at[s, c, side],
-            dst_ref=inbox.at[s, c, side],
-            send_sem=halo_send.at[s, c, side],
-            recv_sem=halo_recv.at[s, c, side],
-            device_id={"space": to},
-            device_id_type=MESH,
-        )
-
-    sends = (me < n_space - 1, me > 0)
+    sides = []
+    for k in range(2):
+        side = lax.rem(me + 1 + k, 2)
+        to = me + 1 - 2 * side
+        sides.append((side, to, jnp.logical_and(to >= 0, to < n_space)))
     takes = (me > 0, me < n_space - 1)
 
     def send(s, c):
-        for side in range(2):
-            pl.when(sends[side])(passed(s, c, side).start)
+        for side, to, there in sides:
+            pl.when(there)(
+                pltpu.make_async_remote_copy(
+                    src_ref=outbox.at[s, c, side],
+                    dst_ref=inbox.at[s, c, side],
+                    send_sem=halo_send,
+                    recv_sem=halo_recv.at[s, c, side],
+                    device_id={"space": to},
+                    device_id_type=MESH,
+                ).start
+            )
 
     def take(s, c):
         for side in range(2):
-            pl.when(takes[side])(passed(s, c, side).wait_recv)
+            came = inbox.at[s, c, side]
+            pl.when(takes[side])(pltpu.make_async_copy(came, came, halo_recv.at[s, c, side]).wait)
 
     moves = [
         pltpu.make_async_remote_copy(
@@ -172,15 +179,14 @@
         rounded[0, :, :, span(c)] = first.reshape(aggs, size, cols)
         outbox[0, c] = dot(picks[...], first).astype(bf16).reshape(2, halo, cols)
         if c == 0:
-            pl.semaphore_wait(barrier, greeted + n_src - 1)
+            pl.semaphore_wait(barrier, count(1) + n_src - 1)
         send(0, c)
         if c == 0:
             for move in moves:
                 move.start()
-        red[me, 0:1, span(c)] = jnp.sum(right * right, axis=0, keepdims=True)
-
-    if hears:
-        hear()
+        red[me, c : c + 1, :] = jnp.sum(right * right, axis=0, keepdims=True).astype(red.dtype)
+
+    tell()
     nbr_load.wait()
     for load in own:
         load.wait()
@@ -191,13 +197,16 @@
 
     def local_part(c, now, later, keep, gain):
         wide = span(c, GROUP)
-        ready = []
+        inner = []
         for a in range(aggs):
             beside = [rounded[now, a, :, wide]]
             for k in range(nbrs):
                 beside.append(rounded[now, nbr_ref[k, a], :, wide])
             left = res[rows(a), wide] - dot(weights[a], jnp.concatenate(beside, axis=0))
-            res[rows(a), wide] = left
+            if keep is not None or not 0 < a < aggs - 1:
+                res[rows(a), wide] = left
+            else:
+                inner.append(jnp.sum(left * left, axis=0, keepdims=True))
             if keep is not None:
                 onward = keep * dirn[rows(a), wide] + gain * left
                 dirn[rows(a), wide] = onward
@@ -206,6 +215,8 @@
                     total[rows(a), wide] += onward
         if keep is not None:
             ahead[:, wide] = dot(picks[...], rounded[later, :, :, wide].reshape(edges, GROUP * cols))
+        else:
+            ahead[0:1, wide] = sum(inner, jnp.zeros((1, GROUP * cols), f32))
 
     def halo_part(s, c, later, gain):
         take(s, c)
@@ -224,28 +235,24 @@
     steps = sweep_weights()
     for c in range(0, CHUNKS, GROUP):
         local_part(c, 0, 1, *steps[0])
-    if hears:
-        hear()
+    tell()
     for s in range(SWEEPS - 1):
         for c in range(CHUNKS):
             halo_part(s, c, (s + 1) % 2, steps[s][1])
             if (c + 1) % GROUP == 0:
                 local_part(c + 1 - GROUP, (s + 1) % 2, s % 2, *(steps[s + 1] if s + 2 < SWEEPS else (None, None)))
-
-    while hears:
-        hear()
+            if c % 2 == 1:
+                tell()
+
+    while len(told) <= levels:
+        tell()
     for c in range(CHUNKS):
         take(SWEEPS - 1, c)
-        squares = jnp.zeros((1, cols), f32)
-        for a in range(aggs):
-            left = res[rows(a), span(c)]
-            for side, b in ((0, 0), (1, aggs - 1)):
-                if a == b:
-                    left = left - dot(gmat[side], inbox[SWEEPS - 1, c, side])
+        squares = ahead[0:1, span(c)]
+        for side, a in ((0, 0), (1, aggs - 1)):
+            left = res[rows(a), span(c)] - dot(gmat[side], inbox[SWEEPS - 1, c, side])
             squares = squares + jnp.sum(left * left, axis=0, keepdims=True)
-        red[me, 1:2, span(c)] = squares
-    if last_heard is not None:
-        pl.semaphore_wait(heard.at[last_heard], 1)
+        red[me, CHUNKS + c : CHUNKS + c + 1, :] = squares.astype(red.dtype)
 
     def share(k, carry):
         pltpu.make_async_remote_copy(
@@ -253,20 +260,19 @@
             dst_ref=red.at[me],
             send_sem=sums_send,
             recv_sem=sums_recv,
-            device_id={"space": lax.rem(me + k, n_space)},
+            device_id={"space": k + (k >= me).astype(jnp.int32)},
             device_id_type=MESH,
         ).start()
         return carry
 
-    lax.fori_loop(1, n_space, share, 0)
-    for s in range(SWEEPS):
-        for c in range(CHUNKS):
-            for side in range(2):
-                pl.when(sends[side])(passed(s, c, side).wait_send)
+    lax.fori_loop(0, n_space - 1, share, 0)
+    for _, _, there in sides:
+        sent = outbox.at[:, :, 0]
+        pl.when(there)(pltpu.make_async_copy(sent, sent, halo_send).wait)
     others = red.at[pl.ds(0, n_space - 1)]
     pltpu.make_async_copy(others, others, sums_recv).wait()
-    sums = jnp.sum(red[...], axis=0)
-    misfit_ref[...] = jnp.sqrt(sums[1:2] / (sums[0:1] + 1e-06))
+    sums = jnp.sum(red[...].astype(f32), axis=0)
+    misfit_ref[...] = jnp.sqrt(sums[CHUNKS:] / (sums[:CHUNKS] + 1e-06))
     pltpu.make_async_copy(others, others, sums_send).wait()
 
 
@@ -278,7 +284,9 @@
     ]
     for copy in copies:
         copy.start()
-    flat[...] = misfit_ref[0, :]
+    chunks, cols = misfit_ref.shape
+    for c in range(chunks):
+        flat[pl.ds(c * cols, cols)] = misfit_ref[c, :]
     copies.append(pltpu.make_async_copy(flat, misfit_out, sems.at[CHUNKS]))
     copies[-1].start()
     for copy in copies:
@@ -299,7 +307,7 @@
         functools.partial(kernel, n_space, n_src),
         out_shape=(
             pltpu.VMEM((edges, width), f32),
-            pltpu.VMEM((1, width), f32),
+            pltpu.VMEM((CHUNKS, cols), f32),
         ),
         in_specs=[outside] * 6,
         out_specs=(inside, inside),
@@ -316,18 +324,18 @@
             pltpu.SMEM((nbrs, aggs), jnp.int32),
             pltpu.VMEM((SWEEPS, CHUNKS, 2, halo, cols), bf16),
             pltpu.VMEM((SWEEPS, CHUNKS, 2, halo, cols), bf16),
-            pltpu.VMEM((n_space, 2, width), f32),
+            pltpu.VMEM((n_space, 2 * CHUNKS, cols), f32),
             dma((CHUNKS,)),
             dma,
             dma,
             dma((nbrs + 2,)),
             dma((max(n_src - 1, 1), nbrs + 2)),
             dma((max(n_src - 1, 1), nbrs + 2)),
+            dma,
             dma((SWEEPS, CHUNKS, 2)),
-            dma((SWEEPS, CHUNKS, 2)),
-            dma,
-            dma,
-            pltpu.SemaphoreType.REGULAR((max(n_space.bit_length() - 1, 1),)),
+            dma,
+            dma,
+            pltpu.SemaphoreType.REGULAR((max((n_space - 1).bit_length(), 1),)),
         ],
         compiler_params=pltpu.CompilerParams(
             collective_id=0, has_side_effects=True, vmem_limit_bytes=(60 << 20) - edges * width * 4

time: 37.3 us -> 37 us (level)
  Pallas kernels: 36.5 us -> 36 us
    pallas_call x1, Pallas kernels: 35.3 us -> 34.9 us  [local(): pl.pallas_call(functools.partial(kernel, n_space, n_src), out_shape=(pltp...]
where the time goes in v2:
time: 37 us; the launch traced here: 36.8 us
  Pallas kernels  36 us (97%)
  between operations  0.8 us (2%)
    pallas_call x1, Pallas kernels, local(): pl.pallas_call(functools.partial(kernel, n_space, n_src), out_shape=(pltp...  34.9 us
    pallas_call x1, Pallas kernels, local(): pl.pallas_call(store, out_shape=(jax.ShapeDtypeStruct((edges, width), f32...  1.18 us

profile of v2, /device:TPU:0, one launch (start us, length us, event | category | flops | bytes accessed | tf_op | source)
XLA Modules:
  0.0 36.8 jit_solution(3687556745863663073)
XLA Ops:
  0.6 34.9 %shard_map.77 = (f32[768,512]{1,0:T(8,128)S(1)}, f32[4,128]{1,0:T(4,128)S(1)}) custom-call(f32[768,512]{1,0:T(8,128)} %rhs_ref.1, bf16[3,128,256]{2,1,0:T(8,128)(2,1)} %diag_ref.1, bf16[3,2,128,256]{3,2,1,0:T(8,128)(2,1)} %couple_ref.1, bf16[2,128,128]{2,1,0:T(8,128)(2,1)} %halo_ref.1, s32[2,3]{1,0:T(2,128)} %bitcast.1, s32[2,128]{1,0:T(2,128)} %bnd_ref.1), custom_call_target="tpu_custom_call" | custom-call | tf_op jit(solution)/shard_map/pallas_call | solution.py:306
  35.5 1.2 %shard_map.78 = (f32[768,512]{1,0:T(8,128)}, f32[512]{0:T(512)}) custom-call(f32[768,512]{1,0:T(8,128)S(1)} %get-tuple-element.4.total, f32[4,128]{1,0:T(4,128)S(1)} %get-tuple-element.5.misfit_ref), custom_call_target="tpu_custom_call" | custom-call | tf_op jit(solution)/shard_map/pallas_call | solution.py:344

commit v3 on v2

--- a/solution.py
+++ b/solution.py
@@ -9,7 +9,8 @@
 
 SWEEPS = 4
 CHUNKS = 4
-GROUP = 1
+GROUP = 2
+FIRST = 2
 MESH = pl.DeviceIdType.MESH
 
 centre = 4.0
@@ -138,9 +139,11 @@
         sides.append((side, to, jnp.logical_and(to >= 0, to < n_space)))
     takes = (me > 0, me < n_space - 1)
 
-    def send(s, c):
+    even = lax.rem(core, 2) == 0
+
+    def send(s, c, when=True):
         for side, to, there in sides:
-            pl.when(there)(
+            pl.when(jnp.logical_and(there, when))(
                 pltpu.make_async_remote_copy(
                     src_ref=outbox.at[s, c, side],
                     dst_ref=inbox.at[s, c, side],
@@ -195,8 +198,8 @@
     for side, a in ((0, 0), (1, aggs - 1)):
         spread[:, pl.ds(side * halo, halo)] = dot(picks[:, rows(a)], gmat[side]).astype(bf16)
 
-    def local_part(c, now, later, keep, gain):
-        wide = span(c, GROUP)
+    def local_part(c, many, now, later, keep, gain):
+        wide = span(c, many)
         inner = []
         for a in range(aggs):
             beside = [rounded[now, a, :, wide]]
@@ -214,16 +217,16 @@
                 if 0 < a < aggs - 1:
                     total[rows(a), wide] += onward
         if keep is not None:
-            ahead[:, wide] = dot(picks[...], rounded[later, :, :, wide].reshape(edges, GROUP * cols))
+            ahead[:, wide] = dot(picks[...], rounded[later, :, :, wide].reshape(edges, many * cols))
         else:
-            ahead[0:1, wide] = sum(inner, jnp.zeros((1, GROUP * cols), f32))
+            ahead[0:1, wide] = sum(inner, jnp.zeros((1, many * cols), f32))
 
     def halo_part(s, c, later, gain):
         take(s, c)
         came = inbox[s, c].reshape(2 * halo, cols)
         onward = ahead[:, span(c)] - gain * dot(spread[...], came)
         outbox[s + 1, c] = onward.astype(bf16).reshape(2, halo, cols)
-        send(s + 1, c)
+        send(s + 1, c, even)
         for side, a in ((0, 0), (1, aggs - 1)):
             pushed = dot(gmat[side], inbox[s, c, side])
             res[rows(a), span(c)] -= pushed
@@ -233,14 +236,17 @@
             rounded[later, a, :, span(c)] = step.astype(bf16)
 
     steps = sweep_weights()
-    for c in range(0, CHUNKS, GROUP):
-        local_part(c, 0, 1, *steps[0])
+    for c in range(0, CHUNKS, FIRST):
+        local_part(c, FIRST, 0, 1, *steps[0])
     tell()
     for s in range(SWEEPS - 1):
         for c in range(CHUNKS):
             halo_part(s, c, (s + 1) % 2, steps[s][1])
             if (c + 1) % GROUP == 0:
-                local_part(c + 1 - GROUP, (s + 1) % 2, s % 2, *(steps[s + 1] if s + 2 < SWEEPS else (None, None)))
+                local_part(c + 1 - GROUP, GROUP, (s + 1) % 2, s % 2, *(steps[s + 1] if s + 2 < SWEEPS else (None, None)))
+            if (c + 1) % GROUP == 0:
+                for d in range(c + 1 - GROUP, c + 1):
+                    send(s + 1, d, jnp.logical_not(even))
             if c % 2 == 1:
                 tell()
 

time: 37 us -> 36.5 us (0.986)
  the two profiles are of different devices: /device:TPU:0 before, /device:TPU:1 now
where the time goes in v3:
time: 36.5 us; the launch traced here: 36.3 us
  Pallas kernels  35.7 us (98%)
  between operations  0.64 us (2%)
    pallas_call x1, Pallas kernels, local(): pl.pallas_call(functools.partial(kernel, n_space, n_src), out_shape=(pltp...  34.5 us
    pallas_call x1, Pallas kernels, local(): pl.pallas_call(store, out_shape=(jax.ShapeDtypeStruct((edges, width), f32...  1.18 us

profile of v3, /device:TPU:1, one launch (start us, length us, event | category | flops | bytes accessed | tf_op | source)
XLA Modules:
  0.0 36.3 jit_solution(10679640312921912707)
XLA Ops:
  0.6 34.5 %shard_map.77 = (f32[768,512]{1,0:T(8,128)S(1)}, f32[4,128]{1,0:T(4,128)S(1)}) custom-call(f32[768,512]{1,0:T(8,128)} %rhs_ref.1, bf16[3,128,256]{2,1,0:T(8,128)(2,1)} %diag_ref.1, bf16[3,2,128,256]{3,2,1,0:T(8,128)(2,1)} %couple_ref.1, bf16[2,128,128]{2,1,0:T(8,128)(2,1)} %halo_ref.1, s32[2,3]{1,0:T(2,128)} %bitcast.1, s32[2,128]{1,0:T(2,128)} %bnd_ref.1), custom_call_target="tpu_custom_call" | custom-call | tf_op jit(solution)/shard_map/pallas_call | solution.py:312
  35.1 1.2 %shard_map.78 = (f32[768,512]{1,0:T(8,128)}, f32[512]{0:T(512)}) custom-call(f32[768,512]{1,0:T(8,128)S(1)} %get-tuple-element.4.total, f32[4,128]{1,0:T(4,128)S(1)} %get-tuple-element.5.misfit_ref), custom_call_target="tpu_custom_call" | custom-call | tf_op jit(solution)/shard_map/pallas_call | solution.py:350

commit v4 on v3

--- a/solution.py
+++ b/solution.py
@@ -226,7 +226,7 @@
         came = inbox[s, c].reshape(2 * halo, cols)
         onward = ahead[:, span(c)] - gain * dot(spread[...], came)
         outbox[s + 1, c] = onward.astype(bf16).reshape(2, halo, cols)
-        send(s + 1, c, even)
+        send(s + 1, c, True if s + 2 == SWEEPS else even)
         for side, a in ((0, 0), (1, aggs - 1)):
             pushed = dot(gmat[side], inbox[s, c, side])
             res[rows(a), span(c)] -= pushed
@@ -245,7 +245,7 @@
             if (c + 1) % GROUP == 0:
                 local_part(c + 1 - GROUP, GROUP, (s + 1) % 2, s % 2, *(steps[s + 1] if s + 2 < SWEEPS else (None, None)))
             if (c + 1) % GROUP == 0:
-                for d in range(c + 1 - GROUP, c + 1):
+                for d in range(c + 1 - GROUP, c + 1 if s + 2 < SWEEPS else 0):
                     send(s + 1, d, jnp.logical_not(even))
             if c % 2 == 1:
                 tell()

time: 36.5 us -> 36.3 us (level)
  the two profiles are of different devices: /device:TPU:1 before, /device:TPU:0 now
where the time goes in v4:
time: 36.3 us; the launch traced here: 35.5 us
  Pallas kernels  34.9 us (96%)
  between operations  0.64 us (2%)
    pallas_call x1, Pallas kernels, local(): pl.pallas_call(functools.partial(kernel, n_space, n_src), out_shape=(pltp...  33.7 us
    pallas_call x1, Pallas kernels, local(): pl.pallas_call(store, out_shape=(jax.ShapeDtypeStruct((edges, width), f32...  1.18 us

profile of v4, /device:TPU:0, one launch (start us, length us, event | category | flops | bytes accessed | tf_op | source)
XLA Modules:
  0.0 35.5 jit_solution(4026993774214510467)
XLA Ops:
  0.6 33.7 %shard_map.77 = (f32[768,512]{1,0:T(8,128)S(1)}, f32[4,128]{1,0:T(4,128)S(1)}) custom-call(f32[768,512]{1,0:T(8,128)} %rhs_ref.1, bf16[3,128,256]{2,1,0:T(8,128)(2,1)} %diag_ref.1, bf16[3,2,128,256]{3,2,1,0:T(8,128)(2,1)} %couple_ref.1, bf16[2,128,128]{2,1,0:T(8,128)(2,1)} %halo_ref.1, s32[2,3]{1,0:T(2,128)} %bitcast.1, s32[2,128]{1,0:T(2,128)} %bnd_ref.1), custom_call_target="tpu_custom_call" | custom-call | tf_op jit(solution)/shard_map/pallas_call | solution.py:312
  34.4 1.2 %shard_map.78 = (f32[768,512]{1,0:T(8,128)}, f32[512]{0:T(512)}) custom-call(f32[768,512]{1,0:T(8,128)S(1)} %get-tuple-element.4.total, f32[4,128]{1,0:T(4,128)S(1)} %get-tuple-element.5.misfit_ref), custom_call_target="tpu_custom_call" | custom-call | tf_op jit(solution)/shard_map/pallas_call | solution.py:350

commit v5 on v4

--- a/solution.py
+++ b/solution.py
@@ -244,9 +244,13 @@
             halo_part(s, c, (s + 1) % 2, steps[s][1])
             if (c + 1) % GROUP == 0:
                 local_part(c + 1 - GROUP, GROUP, (s + 1) % 2, s % 2, *(steps[s + 1] if s + 2 < SWEEPS else (None, None)))
-            if (c + 1) % GROUP == 0:
-                for d in range(c + 1 - GROUP, c + 1 if s + 2 < SWEEPS else 0):
-                    send(s + 1, d, jnp.logical_not(even))
+            if (c + 1) % GROUP == 0 and s + 2 < SWEEPS:
+
+                @pl.when(jnp.logical_not(even))
+                def _():
+                    for d in range(c + 1 - GROUP, c + 1):
+                        send(s + 1, d)
+
             if c % 2 == 1:
                 tell()
 

time: 36.3 us -> 36.3 us (level)
  no operation moved by 1% of the time
where the time goes in v5:
time: 36.3 us; the launch traced here: 35.5 us
  Pallas kernels  34.9 us (96%)
  between operations  0.64 us (2%)
    pallas_call x1, Pallas kernels, local(): pl.pallas_call(functools.partial(kernel, n_space, n_src), out_shape=(pltp...  33.7 us
    pallas_call x1, Pallas kernels, local(): pl.pallas_call(store, out_shape=(jax.ShapeDtypeStruct((edges, width), f32...  1.18 us

profile of v5, /device:TPU:0, one launch (start us, length us, event | category | flops | bytes accessed | tf_op | source)
XLA Modules:
  0.0 35.5 jit_solution(4026993774214510467)
XLA Ops:
  0.6 33.7 %shard_map.77 = (f32[768,512]{1,0:T(8,128)S(1)}, f32[4,128]{1,0:T(4,128)S(1)}) custom-call(f32[768,512]{1,0:T(8,128)} %rhs_ref.1, bf16[3,128,256]{2,1,0:T(8,128)(2,1)} %diag_ref.1, bf16[3,2,128,256]{3,2,1,0:T(8,128)(2,1)} %couple_ref.1, bf16[2,128,128]{2,1,0:T(8,128)(2,1)} %halo_ref.1, s32[2,3]{1,0:T(2,128)} %bitcast.1, s32[2,128]{1,0:T(2,128)} %bnd_ref.1), custom_call_target="tpu_custom_call" | custom-call | tf_op jit(solution)/shard_map/pallas_call | solution.py:316
  34.4 1.2 %shard_map.78 = (f32[768,512]{1,0:T(8,128)}, f32[512]{0:T(512)}) custom-call(f32[768,512]{1,0:T(8,128)S(1)} %get-tuple-element.4.total, f32[4,128]{1,0:T(4,128)S(1)} %get-tuple-element.5.misfit_ref), custom_call_target="tpu_custom_call" | custom-call | tf_op jit(solution)/shard_map/pallas_call | solution.py:354
